TPU v7x, 256 devices: a whole 4x4x8 slice. The times are simulated.
256 devices in a mesh: seq: 32 (over z, x_lo, core), head: 8 (over x_hi, y).
Axes of the slice: x: 4 (x_hi: 2, x_lo: 2; x = x_hi * 2 + x_lo), y: 4, z: 8, core: 2. Of those that a mesh axis runs over, the one named last changes fastest.
Arguments:
- tokens: bfloat16 [16384, 2048], P('seq', 'head'), may hold values from -6 to 6
- norm_gain: float32 [2048], replicated, may hold values from 0.25 to 1.75
- w_qkv: bfloat16 [3, 2048, 2048], P(None, None, 'head'), may hold values from -0.125 to 0.125
- head_scale: float32 [16], P('head'), may hold values from 4 to 24
- w_out: bfloat16 [2048, 2048], P('head'), may hold values from -0.25 to 0.25
- scale_ids: int32 [16384], replicated, may hold values from 0 to 9, as said below
Outputs:
- branch_out: bfloat16 [16384, 2048], P('seq', 'head')
Inputs may be any that keep to these rules, and one draw needn't show every extreme that they name: scale_ids never falls from one token to the next, and every scale from 0 to 9 occurs.
All inputs are finite; a program needn't handle non-finite values.
Results may differ from a plain program's by a relative error of at most 0.014.
Values may be sent and summed in bfloat16 or wider, within the bound.
A program may use at most 128 MiB of HBM per device.

v0:
```python
import math

import jax
import jax.numpy as jnp
from jax import lax
from jax.sharding import PartitionSpec as P


def joined_along(pieces, dim):
    dims = list(pieces.shape[1:])
    dims[dim] *= pieces.shape[0]
    return jnp.moveaxis(pieces, 0, dim).reshape(dims)


def from_everyone(x, axis):
    copies = jnp.broadcast_to(x, (lax.axis_size(axis), *x.shape))
    return lax.all_to_all(copies, axis, split_axis=0, concat_axis=0, tiled=True)


def gather_directly(x, axis, dim):
    return joined_along(from_everyone(x, axis), dim)


def in_one_piece(arrays, axis, dim, along):
    widths = [a.shape[along] for a in arrays]
    both = jnp.concatenate(arrays, axis=along)
    out = lax.all_gather(both, axis, axis=dim, tiled=True)
    return tuple(jnp.split(out, [sum(widths[:k]) for k in range(1, len(widths))], axis=along))


def rms_normed(tokens, norm_gain):
    values = tokens.astype(jnp.float32)
    power = jnp.mean(values * values, axis=-1, keepdims=True)
    return (values * lax.rsqrt(power + 1e-06) * norm_gain).astype(jnp.bfloat16)


def unit_rows(values, factor):
    power = jnp.sum(values * values, axis=-1, keepdims=True)
    return (values * lax.rsqrt(power + 1e-06) * factor).astype(jnp.bfloat16)


def body(tokens, norm_gain, w_qkv, head_scale, w_out, scale_ids):
    rows = tokens.shape[0]
    local_ids = lax.dynamic_slice_in_dim(scale_ids, lax.axis_index("seq") * rows, rows)
    query_top = jnp.max(local_ids)
    wide = gather_directly(tokens, "head", 1)
    normed = rms_normed(wide, norm_gain)
    projected = jnp.einsum("td,cdf->ctf", normed, w_qkv, preferred_element_type=jnp.float32)
    local_heads = head_scale.shape[0]
    head_size = projected.shape[2] // local_heads
    query_n = unit_rows(
        projected[0].reshape(rows, local_heads, head_size), head_scale[None, :, None]
    )
    key_n = unit_rows(projected[1].reshape(rows, local_heads, head_size), 1.0)
    val_b = projected[2].reshape(rows, local_heads, head_size).astype(jnp.bfloat16)
    start_top = jnp.full((local_heads, rows), -1e30, jnp.float32)
    start_total = jnp.zeros((local_heads, rows), jnp.float32)
    start_acc = jnp.zeros((rows, local_heads, head_size), jnp.float32)
    keys, vals = in_one_piece((key_n, val_b), "seq", 0, 1)
    count = keys.shape[0]
    ksize = math.gcd(count, 2048)
    kcount = count // ksize
    key_blocks = keys.reshape(kcount, ksize, local_heads, head_size)
    val_blocks = vals.reshape(kcount, ksize, local_heads, head_size)
    block_starts = jnp.arange(kcount, dtype=jnp.int32) * ksize

    def step(state, blk):
        kblk, vblk, offset = blk
        kid = lax.dynamic_slice_in_dim(scale_ids, offset, ksize)

        def update(st):
            tops, totals, accs = st
            score = jnp.einsum("qhd,khd->hqk", query_n, kblk, preferred_element_type=jnp.float32)
            allowed = (kid[None, :] <= local_ids[:, None])[None]
            score = jnp.where(allowed, score, -1e30)
            new_top = jnp.maximum(tops, jnp.max(score, axis=-1))
            expo = jnp.where(allowed, jnp.exp(score - new_top[:, :, None]), 0.0)
            shrink = jnp.exp(tops - new_top)
            new_total = totals * shrink + jnp.sum(expo, axis=-1)
            summed = jnp.einsum(
                "hqk,khd->qhd", expo.astype(jnp.bfloat16), vblk, preferred_element_type=jnp.float32
            )
            new_acc = accs * jnp.transpose(shrink)[:, :, None] + summed
            return (new_top, new_total, new_acc)

        def keep(st):
            return st

        return (lax.cond(jnp.min(kid) <= query_top, update, keep, state), None)

    result, unused = lax.scan(
        step, (start_top, start_total, start_acc), (key_blocks, val_blocks, block_starts)
    )
    tops, totals, accs = result
    attended = accs / jnp.transpose(totals)[:, :, None]
    attended = attended.reshape(rows, local_heads * head_size).astype(jnp.bfloat16)
    w_cols = lax.all_to_all(w_out, "head", split_axis=1, concat_axis=0, tiled=True)
    return jnp.dot(
        gather_directly(attended, "head", 1), w_cols, preferred_element_type=jnp.float32
    ).astype(jnp.bfloat16)


def solution(mesh):
    placed = (P("seq", "head"), P(), P(None, None, "head"), P("head"), P("head", None), P())
    return jax.shard_map(
        body, mesh=mesh, in_specs=placed, out_specs=P("seq", "head"), check_vma=False
    )
```

profile of v0, /device:TPU:224, one launch (start us, length us, event | category | flops | bytes accessed | tf_op | source)
XLA Modules:
  0.0 357.8 jit_solution(1201002409994441755)
XLA Ops:
  7.8 35.2 %all_to_all.26 = bf16[8,512,256]{2,1,0:T(8,128)(2,1)} all-to-all(bf16[8,512,256]{2,1,0:T(8,128)(2,1)S(1)} %broadcast_in_dim.54), channel_id=1, replica_groups=mesh['seq'=32,'head'=8] {'head'}, dimensions={0} | all-to-all | bytes 4194304 | tf_op jit(solution)/shard_map/all_to_all | solution.py:17
  58.7 4.4 %all-to-all-start.2 = ((bf16[256,8,256]{2,0,1:T(8,128)(2,1)}), bf16[256,8,256]{2,0,1:T(8,128)(2,1)}, u32[]{:S(2)}, u32[]{:S(2)}) async-start(bf16[256,8,256]{2,0,1:T(8,128)(2,1)} %copy.44), calls=%async_computation.2 | async-start | bytes 2097152 | tf_op jit(solution)/shard_map/all_to_all | solution.py:97
  65.1 95.2 %all-gather.2.cloned.1.call-done = bf16[16384,4,128]{2,0,1:T(8,128)(2,1)} async-done(((bf16[512,4,128]{2,0,1:T(8,128)(2,1)}), bf16[16384,4,128]{2,0,1:T(8,128)(2,1)}) %all-gather.2.cloned.1.call-update) | async-done | bytes 16777232 | tf_op jit(solution)/shard_map/all_gather | solution.py:27
  160.3 11.3 %fusion.40 = (bf16[16384,2,128]{2,0,1:T(8,128)(2,1)}, bf16[16384,2,128]{2,0,1:T(8,128)(2,1)}) fusion(bf16[16384,4,128]{2,0,1:T(8,128)(2,1)} %all-gather.2.cloned.1.call-done), kind=kLoop, calls=%fused_computation.47 | loop fusion | bytes 33554432 | tf_op jit(solution)/shard_map/split | solution.py:28
  171.5 7.4 %copy.39 = bf16[8,2048,2,128]{3,1,2,0:T(8,128)(2,1)} copy(bf16[8,2048,2,128]{3,1,0,2:T(8,128)(2,1)} %bitcast.72) | data formatting | bytes 16777216 | tf_op jit(solution)/shard_map/while | solution.py:91
  179.0 7.4 %copy.40 = bf16[8,2048,2,128]{3,1,2,0:T(8,128)(2,1)} copy(bf16[8,2048,2,128]{3,1,0,2:T(8,128)(2,1)} %bitcast.71) | data formatting | bytes 16777216 | tf_op jit(solution)/shard_map/while | solution.py:91
  186.4 124.8 %while.14 = (s32[]{:T(128)}, f32[2,512]{1,0:T(2,128)S(1)}, f32[2,512]{1,0:T(2,128)S(1)}, f32[512,2,128]{2,0,1:T(8,128)S(1)}, s32[8]{0:T(128)S(1)}, /*index=5*/s3...) while((s32[]{:T(128)}, f32[2,512]{1,0:T(2,128)S(1)}, ...), condition=%wide.region_10.11_spmd, body=%wide.region_4.10_spmd.sunk | while | flops 1096029184 | bytes 32861512 | solution.py:91
  192.0 10.0 %conditional.2 = ((f32[2,512]{1,0:T(2,128)S(1)}, f32[2,512]{1,0:T(2,128)S(1)}, f32[512,2,128]{2,0,1:T(8,128)S(1)})) conditional(s32[]{:T(128)} %convert_element_type.70, (f32[2,512]{1,0:T(2,128)S(1)}, f32[2,512]{1,0:T(2,128)S(1)}, f32[512,2,128]{2,0,1:T(8,128)S(1)}) %tuple.42, (s32[2048]{0:T(1024)S(1)}, s32[512]{0:T(512)S(1)}, ...), branch_computations={%region_6.6_spmd, %region_7.9_spmd} | conditional | flops 1096027136 | bytes 32844832 | solution.py:89
  195.6 4.4 %fusion.9 = f32[512,2,128]{2,0,1:T(8,128)S(1)} fusion(f32[2,2048,512]{2,1,0:T(8,128)S(1)} %get-tuple-element.210, f32[2,512]{1,0:T(2,128)S(1)} %get-tuple-element.295, pred[512,2048]{0,1:T(8,128)(4,1)S(1)} %broadcast_compare_fusion, bf16[8,2048,2,128]{3,1,2,0:T(8,128)(2,1)} %get-tuple-element.128, s32[]{:T(128)} %get-tuple-element.124, ...), kind=kOutput, calls=%fused_computation.9 | convolution fusion | flops 545521664 | bytes 11543040 | tf_op jit(solution)/shard_map/while/body/eval_jaxpr/cond/branch_1_fun/hqk,khd->qhd/dot_general | solution.py:80
  207.6 10.0 %conditional.2 = ((f32[2,512]{1,0:T(2,128)S(1)}, f32[2,512]{1,0:T(2,128)S(1)}, f32[512,2,128]{2,0,1:T(8,128)S(1)})) conditional(s32[]{:T(128)} %convert_element_type.70, (f32[2,512]{1,0:T(2,128)S(1)}, f32[2,512]{1,0:T(2,128)S(1)}, f32[512,2,128]{2,0,1:T(8,128)S(1)}) %tuple.42, (s32[2048]{0:T(1024)S(1)}, s32[512]{0:T(512)S(1)}, ...), branch_computations={%region_6.6_spmd, %region_7.9_spmd} | conditional | flops 1096027136 | bytes 32844832 | solution.py:89
  211.2 4.4 %fusion.9 = f32[512,2,128]{2,0,1:T(8,128)S(1)} fusion(f32[2,2048,512]{2,1,0:T(8,128)S(1)} %get-tuple-element.210, f32[2,512]{1,0:T(2,128)S(1)} %get-tuple-element.295, pred[512,2048]{0,1:T(8,128)(4,1)S(1)} %broadcast_compare_fusion, bf16[8,2048,2,128]{3,1,2,0:T(8,128)(2,1)} %get-tuple-element.128, s32[]{:T(128)} %get-tuple-element.124, ...), kind=kOutput, calls=%fused_computation.9 | convolution fusion | flops 545521664 | bytes 11543040 | tf_op jit(solution)/shard_map/while/body/eval_jaxpr/cond/branch_1_fun/hqk,khd->qhd/dot_general | solution.py:80
  223.2 10.0 %conditional.2 = ((f32[2,512]{1,0:T(2,128)S(1)}, f32[2,512]{1,0:T(2,128)S(1)}, f32[512,2,128]{2,0,1:T(8,128)S(1)})) conditional(s32[]{:T(128)} %convert_element_type.70, (f32[2,512]{1,0:T(2,128)S(1)}, f32[2,512]{1,0:T(2,128)S(1)}, f32[512,2,128]{2,0,1:T(8,128)S(1)}) %tuple.42, (s32[2048]{0:T(1024)S(1)}, s32[512]{0:T(512)S(1)}, ...), branch_computations={%region_6.6_spmd, %region_7.9_spmd} | conditional | flops 1096027136 | bytes 32844832 | solution.py:89
  226.8 4.4 %fusion.9 = f32[512,2,128]{2,0,1:T(8,128)S(1)} fusion(f32[2,2048,512]{2,1,0:T(8,128)S(1)} %get-tuple-element.210, f32[2,512]{1,0:T(2,128)S(1)} %get-tuple-element.295, pred[512,2048]{0,1:T(8,128)(4,1)S(1)} %broadcast_compare_fusion, bf16[8,2048,2,128]{3,1,2,0:T(8,128)(2,1)} %get-tuple-element.128, s32[]{:T(128)} %get-tuple-element.124, ...), kind=kOutput, calls=%fused_computation.9 | convolution fusion | flops 545521664 | bytes 11543040 | tf_op jit(solution)/shard_map/while/body/eval_jaxpr/cond/branch_1_fun/hqk,khd->qhd/dot_general | solution.py:80
  238.8 10.0 %conditional.2 = ((f32[2,512]{1,0:T(2,128)S(1)}, f32[2,512]{1,0:T(2,128)S(1)}, f32[512,2,128]{2,0,1:T(8,128)S(1)})) conditional(s32[]{:T(128)} %convert_element_type.70, (f32[2,512]{1,0:T(2,128)S(1)}, f32[2,512]{1,0:T(2,128)S(1)}, f32[512,2,128]{2,0,1:T(8,128)S(1)}) %tuple.42, (s32[2048]{0:T(1024)S(1)}, s32[512]{0:T(512)S(1)}, ...), branch_computations={%region_6.6_spmd, %region_7.9_spmd} | conditional | flops 1096027136 | bytes 32844832 | solution.py:89
  242.4 4.4 %fusion.9 = f32[512,2,128]{2,0,1:T(8,128)S(1)} fusion(f32[2,2048,512]{2,1,0:T(8,128)S(1)} %get-tuple-element.210, f32[2,512]{1,0:T(2,128)S(1)} %get-tuple-element.295, pred[512,2048]{0,1:T(8,128)(4,1)S(1)} %broadcast_compare_fusion, bf16[8,2048,2,128]{3,1,2,0:T(8,128)(2,1)} %get-tuple-element.128, s32[]{:T(128)} %get-tuple-element.124, ...), kind=kOutput, calls=%fused_computation.9 | convolution fusion | flops 545521664 | bytes 11543040 | tf_op jit(solution)/shard_map/while/body/eval_jaxpr/cond/branch_1_fun/hqk,khd->qhd/dot_general | solution.py:80
  254.4 10.0 %conditional.2 = ((f32[2,512]{1,0:T(2,128)S(1)}, f32[2,512]{1,0:T(2,128)S(1)}, f32[512,2,128]{2,0,1:T(8,128)S(1)})) conditional(s32[]{:T(128)} %convert_element_type.70, (f32[2,512]{1,0:T(2,128)S(1)}, f32[2,512]{1,0:T(2,128)S(1)}, f32[512,2,128]{2,0,1:T(8,128)S(1)}) %tuple.42, (s32[2048]{0:T(1024)S(1)}, s32[512]{0:T(512)S(1)}, ...), branch_computations={%region_6.6_spmd, %region_7.9_spmd} | conditional | flops 1096027136 | bytes 32844832 | solution.py:89
  258.0 4.4 %fusion.9 = f32[512,2,128]{2,0,1:T(8,128)S(1)} fusion(f32[2,2048,512]{2,1,0:T(8,128)S(1)} %get-tuple-element.210, f32[2,512]{1,0:T(2,128)S(1)} %get-tuple-element.295, pred[512,2048]{0,1:T(8,128)(4,1)S(1)} %broadcast_compare_fusion, bf16[8,2048,2,128]{3,1,2,0:T(8,128)(2,1)} %get-tuple-element.128, s32[]{:T(128)} %get-tuple-element.124, ...), kind=kOutput, calls=%fused_computation.9 | convolution fusion | flops 545521664 | bytes 11543040 | tf_op jit(solution)/shard_map/while/body/eval_jaxpr/cond/branch_1_fun/hqk,khd->qhd/dot_general | solution.py:80
  270.0 10.0 %conditional.2 = ((f32[2,512]{1,0:T(2,128)S(1)}, f32[2,512]{1,0:T(2,128)S(1)}, f32[512,2,128]{2,0,1:T(8,128)S(1)})) conditional(s32[]{:T(128)} %convert_element_type.70, (f32[2,512]{1,0:T(2,128)S(1)}, f32[2,512]{1,0:T(2,128)S(1)}, f32[512,2,128]{2,0,1:T(8,128)S(1)}) %tuple.42, (s32[2048]{0:T(1024)S(1)}, s32[512]{0:T(512)S(1)}, ...), branch_computations={%region_6.6_spmd, %region_7.9_spmd} | conditional | flops 1096027136 | bytes 32844832 | solution.py:89
  273.6 4.4 %fusion.9 = f32[512,2,128]{2,0,1:T(8,128)S(1)} fusion(f32[2,2048,512]{2,1,0:T(8,128)S(1)} %get-tuple-element.210, f32[2,512]{1,0:T(2,128)S(1)} %get-tuple-element.295, pred[512,2048]{0,1:T(8,128)(4,1)S(1)} %broadcast_compare_fusion, bf16[8,2048,2,128]{3,1,2,0:T(8,128)(2,1)} %get-tuple-element.128, s32[]{:T(128)} %get-tuple-element.124, ...), kind=kOutput, calls=%fused_computation.9 | convolution fusion | flops 545521664 | bytes 11543040 | tf_op jit(solution)/shard_map/while/body/eval_jaxpr/cond/branch_1_fun/hqk,khd->qhd/dot_general | solution.py:80
  285.6 10.0 %conditional.2 = ((f32[2,512]{1,0:T(2,128)S(1)}, f32[2,512]{1,0:T(2,128)S(1)}, f32[512,2,128]{2,0,1:T(8,128)S(1)})) conditional(s32[]{:T(128)} %convert_element_type.70, (f32[2,512]{1,0:T(2,128)S(1)}, f32[2,512]{1,0:T(2,128)S(1)}, f32[512,2,128]{2,0,1:T(8,128)S(1)}) %tuple.42, (s32[2048]{0:T(1024)S(1)}, s32[512]{0:T(512)S(1)}, ...), branch_computations={%region_6.6_spmd, %region_7.9_spmd} | conditional | flops 1096027136 | bytes 32844832 | solution.py:89
  289.2 4.4 %fusion.9 = f32[512,2,128]{2,0,1:T(8,128)S(1)} fusion(f32[2,2048,512]{2,1,0:T(8,128)S(1)} %get-tuple-element.210, f32[2,512]{1,0:T(2,128)S(1)} %get-tuple-element.295, pred[512,2048]{0,1:T(8,128)(4,1)S(1)} %broadcast_compare_fusion, bf16[8,2048,2,128]{3,1,2,0:T(8,128)(2,1)} %get-tuple-element.128, s32[]{:T(128)} %get-tuple-element.124, ...), kind=kOutput, calls=%fused_computation.9 | convolution fusion | flops 545521664 | bytes 11543040 | tf_op jit(solution)/shard_map/while/body/eval_jaxpr/cond/branch_1_fun/hqk,khd->qhd/dot_general | solution.py:80
  301.2 10.0 %conditional.2 = ((f32[2,512]{1,0:T(2,128)S(1)}, f32[2,512]{1,0:T(2,128)S(1)}, f32[512,2,128]{2,0,1:T(8,128)S(1)})) conditional(s32[]{:T(128)} %convert_element_type.70, (f32[2,512]{1,0:T(2,128)S(1)}, f32[2,512]{1,0:T(2,128)S(1)}, f32[512,2,128]{2,0,1:T(8,128)S(1)}) %tuple.42, (s32[2048]{0:T(1024)S(1)}, s32[512]{0:T(512)S(1)}, ...), branch_computations={%region_6.6_spmd, %region_7.9_spmd} | conditional | flops 1096027136 | bytes 32844832 | solution.py:89
  304.8 4.4 %fusion.9 = f32[512,2,128]{2,0,1:T(8,128)S(1)} fusion(f32[2,2048,512]{2,1,0:T(8,128)S(1)} %get-tuple-element.210, f32[2,512]{1,0:T(2,128)S(1)} %get-tuple-element.295, pred[512,2048]{0,1:T(8,128)(4,1)S(1)} %broadcast_compare_fusion, bf16[8,2048,2,128]{3,1,2,0:T(8,128)(2,1)} %get-tuple-element.128, s32[]{:T(128)} %get-tuple-element.124, ...), kind=kOutput, calls=%fused_computation.9 | convolution fusion | flops 545521664 | bytes 11543040 | tf_op jit(solution)/shard_map/while/body/eval_jaxpr/cond/branch_1_fun/hqk,khd->qhd/dot_general | solution.py:80
  311.8 36.6 %all_to_all.27 = bf16[8,512,256]{2,1,0:T(8,128)(2,1)S(1)} all-to-all(bf16[8,512,256]{2,1,0:T(8,128)(2,1)S(1)} %broadcast_in_dim.55), channel_id=1, replica_groups=mesh['seq'=32,'head'=8] {'head'}, dimensions={0} | all-to-all | bytes 4194304 | tf_op jit(solution)/shard_map/all_to_all | solution.py:17
  (109 shorter events, 83.5 us)
Async XLA Ops:
  6.5 44.7 %copy-start = (bf16[3,2048,256]{2,1,0:T(8,128)(2,1)S(1)}, bf16[3,2048,256]{2,1,0:T(8,128)(2,1)}, u32[]{:S(2)}) copy-start(bf16[3,2048,256]{2,1,0:T(8,128)(2,1)} %param.12) | copy-start | bytes 9437188
  6.5 153.7 %all-gather.2.cloned.1.call-start = ((), (), s32[]{:S(2)}) async-start(), calls=%async_computation.3 | async-start | bytes 17301504 | tf_op jit(solution)/shard_map/all_gather | solution.py:27
  43.0 6.1 %copy-start.4 = (f32[2048]{0:T(1024)S(1)}, f32[2048]{0:T(1024)}, u32[]{:S(2)}) copy-start(f32[2048]{0:T(1024)} %param.11) | copy-start | bytes 24580
  53.0 1.2 copy-start.2
  53.1 3.8 %copy-start.3 = (bf16[256,2048]{1,0:T(8,128)(2,1)S(1)}, bf16[256,2048]{1,0:T(8,128)(2,1)}, u32[]{:S(2)}) copy-start(bf16[256,2048]{1,0:T(8,128)(2,1)} %param.14) | copy-start | bytes 3145732
  56.8 8.1 %copy-start.5 = (f32[2]{0:T(128)S(1)}, f32[2]{0:T(128)}, u32[]{:S(2)}) copy-start(f32[2]{0:T(128)} %param.13) | copy-start | bytes 28
  58.7 252.9 %all-to-all-start.2 = ((bf16[256,8,256]{2,0,1:T(8,128)(2,1)}), bf16[256,8,256]{2,0,1:T(8,128)(2,1)}, u32[]{:S(2)}, u32[]{:S(2)}) async-start(bf16[256,8,256]{2,0,1:T(8,128)(2,1)} %copy.44), calls=%async_computation.2 | async-start | bytes 2097152 | tf_op jit(solution)/shard_map/all_to_all | solution.py:97
  311.6 39.4 %copy-start.1 = (bf16[3,2048,256]{2,1,0:T(8,128)(2,1)S(1)}, bf16[3,2048,256]{2,1,0:T(8,128)(2,1)}, u32[]{:S(2)}) copy-start(bf16[3,2048,256]{2,1,0:T(8,128)(2,1)} %param.12) | copy-start | bytes 9437188
Sparse Core Ops, SparseCore 0:
  56.9 103.2 all-gather.1
where the time goes:
time: 360 us; the launch traced here: 358 us
  waiting for transfers between devices  95.2 us (26%)
  blocking collectives  71.8 us (20%)
  matrix products  61.6 us (17%)
  local copies, waits for them, and re-layouts  41.7 us (12%)
  other arithmetic  41.2 us (11%)
  loops' own time  28.2 us (8%)
  between operations  13.6 us (4%)
  starting transfers between devices  4.43 us (1%)
    all_gather x1, waiting for transfers between devices, in_one_piece(): out = lax.all_gather(both, axis, axis=dim, tiled=True)  95.2 us
    all_to_all x2, blocking collectives, from_everyone(): return lax.all_to_all(copies, axis, split_axis=0, concat_axis=0, tiled=True)  71.8 us
    dot_general x8, matrix products, update(): jnp.einsum('hqk,khd->qhd', expo.astype(jnp.bfloat16), vblk, preferred_ele...  35.1 us
    another operation x1, loops' own time, body(): lax.scan(step, (start_top, start_total, start_acc), (key_blocks, val_bloc...  27.8 us
    dot_general x8, matrix products, update(): jnp.einsum('qhd,khd->hqk', query_n, kblk, preferred_element_type=jnp.floa...  22.1 us
    reduce_sum x8, other arithmetic, update(): new_total = totals * shrink + jnp.sum(expo, axis=-1)  15.7 us
    while x3, local copies, waits for them, and re-layouts, body(): lax.scan(step, (start_top, start_total, start_acc), (key_blocks, val_bloc...  15 us
    reduce_min x8, other arithmetic, step(): return (lax.cond(jnp.min(kid) <= query_top, update, keep, state), None)  12 us
  transfers between devices with their start and end apart: 2, of which 1 were waited for; matrix products, arithmetic and copies ran while one was open for 35% of the time, Pallas kernels for 0%

commit v1 on v0

v1 whole, which is shorter than its diff:
```python
import functools
import math

import jax
import jax.numpy as jnp
from jax import lax
from jax.experimental import pallas as pl
from jax.experimental.pallas import tpu as pltpu
from jax.sharding import PartitionSpec as P

MESH = pl.DeviceIdType.MESH
BF = jnp.bfloat16
F32 = jnp.float32
LOG2E = math.log2(math.e)


def kernel(
    tokens, gain, wqkv, hscale, wout, ids, out,
    xg, wq, acc3, ssq, kv, kvsend, qbuf, qsend, qid, oacc, lacc, attg, osend, wc,
    lsem, gs_x, gr_x, gs_y, gr_y, as_x, ar_x, as_y, ar_y, ws, wr, xs, xr, zs, zr, cs, cr,
):
    rows, feat = tokens.shape
    hd_dim = 128
    sid = lax.axis_index("seq")
    hid = lax.axis_index("head")
    z, xl, c = sid // 4, (sid // 2) % 2, sid % 2
    xh, y = hid // 4, hid % 4

    def sq(zz, xx, cc):
        return lax.rem(zz + 8, 8) * 4 + xx * 2 + cc

    def hx(xx, yy):
        return xx * 4 + lax.rem(yy + 4, 4)

    def at_head(h):
        return (sid, h)

    def at_seq(s):
        return (s, hid)

    x_partner = at_head(hx(1 - xh, y))
    y_up, y_down = at_head(hx(xh, y + 1)), at_head(hx(xh, y - 1))
    pair = at_seq(sq(z, 1 - xl, c))
    twin = at_seq(sq(z, xl, 1 - c))
    z_up, z_down = at_seq(sq(z + 1, xl, c)), at_seq(sq(z - 1, xl, c))

    def remote(src, dst, ssem, rsem, dev):
        return pltpu.make_async_remote_copy(
            src_ref=src, dst_ref=dst, send_sem=ssem, recv_sem=rsem, device_id=dev, device_id_type=MESH
        )

    own = pltpu.make_async_copy(tokens, xg.at[hid], lsem.at[0])
    own.start()
    loads = pltpu.make_async_copy(wqkv, wq, lsem.at[1])
    loads.start()
    own_w = pltpu.make_async_copy(wout.at[:, pl.ds(pl.multiple_of(hid * feat, feat), feat)], wc.at[hid], lsem.at[2])
    own_w.start()

    barrier = pltpu.get_barrier_semaphore()
    for d in range(1, 8):
        pl.semaphore_signal(barrier, inc=1, device_id=at_head(lax.rem(hid + d, 8)), device_id_type=MESH)
    for dev in (pair, twin, z_up, z_down):
        pl.semaphore_signal(barrier, inc=1, device_id=dev, device_id_type=MESH)
    pl.semaphore_wait(barrier, 11)

    pending = []

    def go(copy):
        copy.start()
        pending.append(copy)
        return copy

    def gather(first, buf, sx, rx, sy, ry, consume):
        mine, other = hx(xh, y), hx(1 - xh, y)
        half = rows // 2
        top, bottom = pl.ds(0, half), pl.ds(half, half)
        go(remote(first, buf.at[mine], sx.at[0], rx.at[0], x_partner))
        go(remote(first, buf.at[mine], sy.at[0], ry.at[0], y_up))
        go(remote(first, buf.at[mine], sy.at[1], ry.at[1], y_down))
        remote(first, buf.at[other], sx.at[0], rx.at[0], x_partner).wait_recv()
        go(remote(buf.at[other], buf.at[other], sy.at[2], ry.at[2], y_up))
        go(remote(buf.at[other], buf.at[other], sy.at[3], ry.at[3], y_down))
        for g, xx in ((0, xh), (1, 1 - xh)):
            lo, hi = hx(xx, y - 1), hx(xx, y + 1)
            if g == 0:
                consume(0)
            remote(buf.at[lo], buf.at[lo], sy.at[0], ry.at[2 * g], y_up).wait_recv()
            go(remote(buf.at[lo, top], buf.at[lo, top], sy.at[4 + 2 * g], ry.at[4 + 2 * g], y_up))
            remote(buf.at[hi], buf.at[hi], sy.at[0], ry.at[2 * g + 1], y_down).wait_recv()
            go(remote(buf.at[hi, bottom], buf.at[hi, bottom], sy.at[5 + 2 * g], ry.at[5 + 2 * g], y_down))
            consume(1 + g)
        for g, xx in ((0, xh), (1, 1 - xh)):
            far = hx(xx, y + 2)
            remote(buf.at[far, top], buf.at[far, top], sy.at[4], ry.at[4 + 2 * g], y_up).wait_recv()
            remote(buf.at[far, bottom], buf.at[far, bottom], sy.at[5], ry.at[5 + 2 * g], y_down).wait_recv()
        consume(3)

    def piece_of(stage, i):
        if stage == 0:
            return lax.rem(xh + i, 2) * 4 + y
        if stage == 3:
            return lax.rem(xh + i, 2) * 4 + lax.rem(y + 2, 4)
        g = stage - 1
        return lax.rem(xh + g, 2) * 4 + lax.rem(y + 3 + 2 * i, 4)

    for i in range(2):
        for j in range(4):
            row = ids[pl.ds(sq(z, i, c) * 4 + j, 1), :]
            qid[i, pl.ds(j * 128, 128), :] = jnp.broadcast_to(row.astype(F32), (128, 128)).T
    oacc[...] = jnp.zeros_like(oacc)
    lacc[...] = jnp.zeros_like(lacc)
    acc3[...] = jnp.zeros_like(acc3)
    ssq[...] = jnp.zeros_like(ssq)
    own.wait()
    loads.wait()

    def project(stage):
        def body(i, carry):
            p = piece_of(stage, i)
            lane = pl.ds(pl.multiple_of(p * feat, feat), feat)
            x = xg[p].astype(F32)
            sqv = x * x
            ssq[...] += sqv[:, :128] + sqv[:, 128:]
            xw = (x * gain[:, lane]).astype(BF)
            for j in range(3):
                acc3[:, j * feat:(j + 1) * feat] += jnp.dot(xw, wq[j, lane, :], preferred_element_type=F32)
            return carry

        lax.fori_loop(0, 2, body, 0)

    gather(tokens, xg, gs_x, gr_x, gs_y, gr_y, project)

    r = lax.rsqrt(jnp.sum(ssq[...], axis=-1, keepdims=True) * (1.0 / (8 * feat)) + 1e-06)

    def head_of(j, h):
        return acc3[:, pl.ds(pl.multiple_of(j * feat + h * hd_dim, hd_dim), hd_dim)] * r

    def unit(v, factor):
        power = jnp.sum(v * v, axis=-1, keepdims=True)
        return (v * lax.rsqrt(power + 1e-06) * factor).astype(BF)

    kv[sid, 0] = unit(head_of(1, xl), 1.0)
    kv[sid, 1] = head_of(2, xl).astype(BF)
    go(remote(kv.at[sid], kv.at[sid], zs.at[0, 0], zr.at[0, 0], z_up))
    go(remote(kv.at[sid], kv.at[sid], zs.at[1, 0], zr.at[1, 0], z_down))
    go(remote(kv.at[sid], kv.at[sid], cs.at[2, 0], cr.at[2, 0], twin))
    kvsend[0] = unit(head_of(1, 1 - xl), 1.0)
    kvsend[1] = head_of(2, 1 - xl).astype(BF)
    go(remote(kvsend, kv.at[sid], xs.at[0], xr.at[0], pair))
    qsend[...] = unit(head_of(0, 1 - xl), hscale[0, 1 - xl] * LOG2E)
    go(remote(qsend, qbuf.at[xl], xs.at[1], xr.at[1], pair))
    qbuf[xl] = unit(head_of(0, xl), hscale[0, xl] * LOG2E)
    other = sq(z, 1 - xl, c)
    remote(kvsend, kv.at[other], xs.at[0], xr.at[0], pair).wait_recv()
    go(remote(kv.at[other], kv.at[other], zs.at[0, 1], zr.at[0, 1], z_up))
    go(remote(kv.at[other], kv.at[other], zs.at[1, 1], zr.at[1, 1], z_down))
    go(remote(kv.at[other], kv.at[other], cs.at[2, 1], cr.at[2, 1], twin))

    for d in range(1, 8):
        to = lax.rem(hid + d, 8)
        go(remote(
            wout.at[:, pl.ds(pl.multiple_of(to * feat, feat), feat)], wc.at[hid],
            ws.at[d], wr.at[d], at_head(to),
        ))
    remote(qsend, qbuf.at[1 - xl], xs.at[1], xr.at[1], pair).wait_recv()

    qrows = 256

    def attend(blk):
        k, v = kv[blk, 0], kv[blk, 1]
        kids = [ids[pl.ds(blk * 4 + j, 1), :].astype(F32) for j in range(4)]
        for qb in range(2 * rows // qrows):
            i, lo = divmod(qb * qrows, rows)
            q = qbuf[i, pl.ds(lo, qrows), :]
            s = lax.dot_general(q, k, (((1,), (1,)), ((), ())), preferred_element_type=F32)
            qi = qid[i, pl.ds(lo, qrows), :]
            parts = []
            total = None
            for j in range(4):
                e = jnp.where(kids[j] <= qi, jnp.exp2(s[:, j * 128:(j + 1) * 128]), 0.0)
                total = e if total is None else total + e
                parts.append(e.astype(BF))
            w = jnp.concatenate(parts, axis=1)
            span = pl.ds(lo, qrows)
            oacc[i, span, :] += jnp.dot(w, v, preferred_element_type=F32)
            lacc[i, span, :] += total

    def block_at(dz, u, cc):
        return lax.rem(z + dz + 8, 8) * 4 + lax.rem(xl + u, 2) * 2 + cc

    def loop2(f):
        lax.fori_loop(0, 2, lambda i, carry: (f(i), carry)[1], 0)

    def ring(k, d, dev_step):
        s, u = k // 2 + 1, lax.rem(k, 2)
        blk = block_at(-s if d == 0 else s, u, c)
        remote(kv.at[blk], kv.at[blk], zs.at[d, 0], zr.at[d, k], z_up).wait_recv()
        return blk

    def to_twin(blk, d, k):
        return remote(kv.at[blk], kv.at[blk], cs.at[d, k], cr.at[d, k], twin)

    def from_twin(blk, d, k):
        remote(kv.at[blk], kv.at[blk], cs.at[d, 0], cr.at[d, k], twin).wait_recv()

    loop2(lambda i: attend(block_at(0, i, c)))
    from_twin(block_at(0, 0, 1 - c), 2, 0)
    from_twin(block_at(0, 1, 1 - c), 2, 1)
    loop2(lambda i: attend(block_at(0, i, 1 - c)))

    def lagged(k):
        s, u = k // 2 + 1, lax.rem(k, 2)
        from_twin(block_at(-s, u, 1 - c), 0, k)
        from_twin(block_at(s, u, 1 - c), 1, k)
        loop2(lambda i: attend(block_at((2 * i - 1) * s, u, 1 - c)))

    def period(p, carry):
        s, u = p // 2 + 1, lax.rem(p, 2)
        up = ring(p, 0, z_up)

        @pl.when(p <= 4)
        def _():
            remote(kv.at[up], kv.at[up], zs.at[0, p + 2], zr.at[0, p + 2], z_up).start()

        to_twin(up, 0, p).start()
        down = ring(p, 1, z_down)

        @pl.when(p <= 3)
        def _():
            remote(kv.at[down], kv.at[down], zs.at[1, p + 2], zr.at[1, p + 2], z_down).start()

        @pl.when(p == 5)
        def _():
            remote(kv.at[down], kv.at[down], zs.at[1, p + 2], zr.at[1, p + 2], z_down).start()

        to_twin(down, 1, p).start()
        loop2(lambda i: attend(block_at((2 * i - 1) * s, u, c)))

        @pl.when(p > 0)
        def _():
            lagged(p - 1)

        return carry

    lax.fori_loop(0, 6, period, 0)
    lagged(5)
    last_up = block_at(4, 0, c)
    last_down = block_at(4, 1, c)
    remote(kv.at[last_up], kv.at[last_up], zs.at[0, 0], zr.at[0, 6], z_up).wait_recv()
    go(to_twin(last_up, 0, 6))
    remote(kv.at[last_down], kv.at[last_down], zs.at[1, 0], zr.at[1, 7], z_up).wait_recv()
    go(to_twin(last_down, 1, 7))
    loop2(lambda i: attend(block_at(4, i, c)))
    from_twin(block_at(4, 0, 1 - c), 0, 6)
    from_twin(block_at(4, 1, 1 - c), 1, 7)
    loop2(lambda i: attend(block_at(4, i, 1 - c)))

    def attended(i):
        total = jnp.sum(lacc[i], axis=-1, keepdims=True)
        return (oacc[i] / total).astype(BF)

    osend[...] = attended(1 - xl)
    go(remote(osend, attg.at[hid, xl], xs.at[2], xr.at[2], pair))
    attg[hid, xl] = attended(xl)
    remote(osend, attg.at[hid, 1 - xl], xs.at[2], xr.at[2], pair).wait_recv()

    own_w.wait()
    for d in range(1, 8):
        frm = lax.rem(hid - d + 8, 8)
        remote(wc.at[frm], wc.at[frm], ws.at[d], wr.at[d], at_head(frm)).wait_recv()

    fin = acc3.at[:, pl.ds(0, feat)]

    def finish(stage):
        def body(i, carry):
            p = piece_of(stage, i)
            a = jnp.concatenate([attg[p, 0], attg[p, 1]], axis=1)
            d = jnp.dot(a, wc[p], preferred_element_type=F32)
            fin[...] += d
            return carry

        lax.fori_loop(0, 2, body, 0)

    fin[...] = jnp.zeros((rows, feat), F32)
    gather2(remote, go, attg, hid, hx, xh, y, x_partner, y_up, y_down, as_x, ar_x, as_y, ar_y, finish)
    out[...] = fin[...].astype(BF)

    for k in range(2, 7):
        remote(kv.at[0], kv.at[0], zs.at[0, k], zr.at[0, 0], z_up).wait_send()
    for k in (2, 3, 4, 5, 7):
        remote(kv.at[0], kv.at[0], zs.at[1, k], zr.at[1, 0], z_down).wait_send()
    for k in range(6):
        for d in range(2):
            remote(kv.at[0], kv.at[0], cs.at[d, k], cr.at[d, 0], twin).wait_send()
    for copy in pending:
        copy.wait_send()


def gather2(remote, go, buf, hid, hx, xh, y, x_partner, y_up, y_down, sx, rx, sy, ry, consume):
    mine, other = hx(xh, y), hx(1 - xh, y)
    go(remote(buf.at[mine], buf.at[mine], sx.at[0], rx.at[0], x_partner))
    go(remote(buf.at[mine], buf.at[mine], sy.at[0], ry.at[0], y_up))
    go(remote(buf.at[mine], buf.at[mine], sy.at[1], ry.at[1], y_down))
    remote(buf.at[other], buf.at[other], sx.at[0], rx.at[0], x_partner).wait_recv()
    go(remote(buf.at[other], buf.at[other], sy.at[2], ry.at[2], y_up))
    go(remote(buf.at[other], buf.at[other], sy.at[3], ry.at[3], y_down))
    for g, xx in ((0, xh), (1, 1 - xh)):
        lo, hi = hx(xx, y - 1), hx(xx, y + 1)
        if g == 0:
            consume(0)
        remote(buf.at[lo], buf.at[lo], sy.at[0], ry.at[2 * g], y_up).wait_recv()
        go(remote(buf.at[lo, 0], buf.at[lo, 0], sy.at[4 + 2 * g], ry.at[4 + 2 * g], y_up))
        remote(buf.at[hi], buf.at[hi], sy.at[0], ry.at[2 * g + 1], y_down).wait_recv()
        go(remote(buf.at[hi, 1], buf.at[hi, 1], sy.at[5 + 2 * g], ry.at[5 + 2 * g], y_down))
        consume(1 + g)
    for g, xx in ((0, xh), (1, 1 - xh)):
        far = hx(xx, y + 2)
        remote(buf.at[far, 0], buf.at[far, 0], sy.at[4], ry.at[4 + 2 * g], y_up).wait_recv()
        remote(buf.at[far, 1], buf.at[far, 1], sy.at[5], ry.at[5 + 2 * g], y_down).wait_recv()
    consume(3)


def body(tokens, norm_gain, w_qkv, head_scale, w_out, scale_ids):
    rows, feat = tokens.shape
    dim = w_qkv.shape[1]
    dma = pltpu.SemaphoreType.DMA
    any_spec = pl.BlockSpec(memory_space=pl.ANY)
    vm = pl.BlockSpec(memory_space=pltpu.VMEM)
    return pl.pallas_call(
        kernel,
        name="branch",
        out_shape=jax.ShapeDtypeStruct((rows, feat), BF),
        in_specs=[any_spec, vm, any_spec, pl.BlockSpec(memory_space=pltpu.SMEM), any_spec, vm],
        out_specs=vm,
        scratch_shapes=[
            pltpu.VMEM((8, rows, feat), BF),
            pltpu.VMEM((3, dim, feat), BF),
            pltpu.VMEM((rows, 3 * feat), F32),
            pltpu.VMEM((rows, 128), F32),
            pltpu.VMEM((32, 2, rows, 128), BF),
            pltpu.VMEM((2, rows, 128), BF),
            pltpu.VMEM((2, rows, 128), BF),
            pltpu.VMEM((rows, 128), BF),
            pltpu.VMEM((2, rows, 128), F32),
            pltpu.VMEM((2, rows, 128), F32),
            pltpu.VMEM((2, rows, 128), F32),
            pltpu.VMEM((8, 2, rows, 128), BF),
            pltpu.VMEM((rows, 128), BF),
            pltpu.VMEM((8, feat, feat), BF),
            dma((3,)),
            dma((1,)), dma((1,)), dma((8,)), dma((8,)),
            dma((1,)), dma((1,)), dma((8,)), dma((8,)),
            dma((8,)), dma((8,)),
            dma((3,)), dma((3,)),
            dma((2, 8)), dma((2, 8)),
            dma((3, 8)), dma((3, 8)),
        ],
        compiler_params=pltpu.CompilerParams(
            collective_id=0, has_side_effects=True, vmem_limit_bytes=56 * 1024 * 1024
        ),
        cost_estimate=pl.CostEstimate(flops=11_000_000_000, bytes_accessed=6_000_000, transcendentals=17_000_000),
    )(tokens, norm_gain.reshape(1, -1), w_qkv, head_scale.reshape(1, -1), w_out, scale_ids.reshape(-1, 128))


def solution(mesh):
    placed = (P("seq", "head"), P(), P(None, None, "head"), P("head"), P("head", None), P())
    return jax.shard_map(
        body, mesh=mesh, in_specs=placed, out_specs=P("seq", "head"), check_vma=False
    )
```

time: 360 us -> 112 us (0.31)
  the two profiles are of different devices: /device:TPU:224 before, /device:TPU:8 now
where the time goes in v1:
time: 112 us
  Pallas kernels  110 us (98%)
  local copies, waits for them, and re-layouts  1.67 us (1%)
    pallas_call x1, Pallas kernels, body(): pl.pallas_call(kernel, name='branch', out_shape=jax.ShapeDtypeStruct((row...  110 us

profile of v1, /device:TPU:8, one launch (start us, length us, event | category | flops | bytes accessed | tf_op | source)
XLA Modules:
  0.0 112.1 jit_solution(1079161008197091545)
XLA Ops:
  0.0 110.4 %branch.1 = bf16[512,256]{1,0:T(8,128)(2,1)} custom-call(bf16[512,256]{1,0:T(8,128)(2,1)} %tokens.1, f32[1,2048]{1,0:T(1,128)} %bitcast.4, bf16[3,2048,256]{2,1,0:T(8,128)(2,1)} %wqkv.1, f32[1,2]{1,0:T(1,128)} %bitcast.5, bf16[256,2048]{1,0:T(8,128)(2,1)} %wout.1, s32[128,128]{1,0:T(8,128)} %bitcast.3), custom_call_target="tpu_custom_call" | custom-call | flops 11000000512 | bytes 6000000 | tf_op jit(solution)/shard_map/branch/pallas_call | solution.py:329
  110.4 1.7 %copy.8 = bf16[512,256]{1,0:T(8,128)(2,1)} copy(bf16[512,256]{1,0:T(8,128)(2,1)} %branch.1) | data formatting | bytes 524288

commit v2 on v1

--- a/solution.py
+++ b/solution.py
@@ -17,7 +17,7 @@
 def kernel(
     tokens, gain, wqkv, hscale, wout, ids, out,
     xg, wq, acc3, ssq, kv, kvsend, qbuf, qsend, qid, oacc, lacc, attg, osend, wc,
-    lsem, gs_x, gr_x, gs_y, gr_y, as_x, ar_x, as_y, ar_y, ws, wr, xs, xr, zs, zr, cs, cr,
+    lsem, gs_x, gr_x, gs_y, gr_y, os, orr, ys, yr, ws, wr, xs, xr, zs, zr, cs, cr,
 ):
     rows, feat = tokens.shape
     hd_dim = 128
@@ -42,6 +42,7 @@
     y_up, y_down = at_head(hx(xh, y + 1)), at_head(hx(xh, y - 1))
     pair = at_seq(sq(z, 1 - xl, c))
     twin = at_seq(sq(z, xl, 1 - c))
+    diag = (sq(z, 1 - xl, c), hx(1 - xh, y))
     z_up, z_down = at_seq(sq(z + 1, xl, c)), at_seq(sq(z - 1, xl, c))
 
     def remote(src, dst, ssem, rsem, dev):
@@ -59,9 +60,9 @@
     barrier = pltpu.get_barrier_semaphore()
     for d in range(1, 8):
         pl.semaphore_signal(barrier, inc=1, device_id=at_head(lax.rem(hid + d, 8)), device_id_type=MESH)
-    for dev in (pair, twin, z_up, z_down):
+    for dev in (pair, twin, diag, z_up, z_down):
         pl.semaphore_signal(barrier, inc=1, device_id=dev, device_id_type=MESH)
-    pl.semaphore_wait(barrier, 11)
+    pl.semaphore_wait(barrier, 12)
 
     pending = []
 
@@ -139,13 +140,19 @@
         power = jnp.sum(v * v, axis=-1, keepdims=True)
         return (v * lax.rsqrt(power + 1e-06) * factor).astype(BF)
 
-    kv[sid, 0] = unit(head_of(1, xl), 1.0)
-    kv[sid, 1] = head_of(2, xl).astype(BF)
+    half = rows // 2
+
+    def store(dst, j, value):
+        dst[0, j] = value[:half]
+        dst[1, j] = value[half:]
+
+    store(kv.at[sid], 0, unit(head_of(1, xl), 1.0))
+    store(kv.at[sid], 1, head_of(2, xl).astype(BF))
     go(remote(kv.at[sid], kv.at[sid], zs.at[0, 0], zr.at[0, 0], z_up))
     go(remote(kv.at[sid], kv.at[sid], zs.at[1, 0], zr.at[1, 0], z_down))
     go(remote(kv.at[sid], kv.at[sid], cs.at[2, 0], cr.at[2, 0], twin))
-    kvsend[0] = unit(head_of(1, 1 - xl), 1.0)
-    kvsend[1] = head_of(2, 1 - xl).astype(BF)
+    store(kvsend, 0, unit(head_of(1, 1 - xl), 1.0))
+    store(kvsend, 1, head_of(2, 1 - xl).astype(BF))
     go(remote(kvsend, kv.at[sid], xs.at[0], xr.at[0], pair))
     qsend[...] = unit(head_of(0, 1 - xl), hscale[0, 1 - xl] * LOG2E)
     go(remote(qsend, qbuf.at[xl], xs.at[1], xr.at[1], pair))
@@ -164,26 +171,25 @@
         ))
     remote(qsend, qbuf.at[1 - xl], xs.at[1], xr.at[1], pair).wait_recv()
 
-    qrows = 256
-
-    def attend(blk):
-        k, v = kv[blk, 0], kv[blk, 1]
+    def attend(blk, parts_of=(0, 1)):
+        k = jnp.concatenate([kv[blk, 0, 0], kv[blk, 1, 0]], axis=0)
+        v = jnp.concatenate([kv[blk, 0, 1], kv[blk, 1, 1]], axis=0)
         kids = [ids[pl.ds(blk * 4 + j, 1), :].astype(F32) for j in range(4)]
-        for qb in range(2 * rows // qrows):
-            i, lo = divmod(qb * qrows, rows)
-            q = qbuf[i, pl.ds(lo, qrows), :]
-            s = lax.dot_general(q, k, (((1,), (1,)), ((), ())), preferred_element_type=F32)
-            qi = qid[i, pl.ds(lo, qrows), :]
-            parts = []
-            total = None
-            for j in range(4):
-                e = jnp.where(kids[j] <= qi, jnp.exp2(s[:, j * 128:(j + 1) * 128]), 0.0)
-                total = e if total is None else total + e
-                parts.append(e.astype(BF))
-            w = jnp.concatenate(parts, axis=1)
-            span = pl.ds(lo, qrows)
-            oacc[i, span, :] += jnp.dot(w, v, preferred_element_type=F32)
-            lacc[i, span, :] += total
+        for qh in parts_of:
+            for i in range(2):
+                span = pl.ds(qh * half, half)
+                q = qbuf[i, span, :]
+                s = lax.dot_general(q, k, (((1,), (1,)), ((), ())), preferred_element_type=F32)
+                qi = qid[i, span, :]
+                parts = []
+                total = None
+                for j in range(4):
+                    e = jnp.where(kids[j] <= qi, jnp.exp2(s[:, j * 128:(j + 1) * 128]), 0.0)
+                    total = e if total is None else total + e
+                    parts.append(e.astype(BF))
+                w = jnp.concatenate(parts, axis=1)
+                oacc[i, span, :] += jnp.dot(w, v, preferred_element_type=F32)
+                lacc[i, span, :] += total
 
     def block_at(dz, u, cc):
         return lax.rem(z + dz + 8, 8) * 4 + lax.rem(xl + u, 2) * 2 + cc
@@ -250,19 +256,34 @@
     go(to_twin(last_up, 0, 6))
     remote(kv.at[last_down], kv.at[last_down], zs.at[1, 0], zr.at[1, 7], z_up).wait_recv()
     go(to_twin(last_down, 1, 7))
-    loop2(lambda i: attend(block_at(4, i, c)))
+    oid = hx(1 - xh, y)
+
+    def hand_out(qh):
+        span = pl.ds(qh * half, half)
+
+        def attended(i):
+            total = jnp.sum(lacc[i, span, :], axis=-1, keepdims=True)
+            return (oacc[i, span, :] / total).astype(BF)
+
+        osend[qh] = attended(1 - xl)
+        mine = attg.at[hid, qh, xl]
+        go(remote(osend.at[qh], mine, os.at[qh, 0], orr.at[qh, 0], pair))
+        go(remote(osend.at[qh], mine, os.at[qh, 1], orr.at[qh, 1], diag))
+        attg[hid, qh, xl] = attended(xl)
+        go(remote(mine, mine, os.at[qh, 2], orr.at[qh, 2], x_partner))
+
+    loop2(lambda i: attend(block_at(4, i, c), (0,)))
     from_twin(block_at(4, 0, 1 - c), 0, 6)
     from_twin(block_at(4, 1, 1 - c), 1, 7)
-    loop2(lambda i: attend(block_at(4, i, 1 - c)))
-
-    def attended(i):
-        total = jnp.sum(lacc[i], axis=-1, keepdims=True)
-        return (oacc[i] / total).astype(BF)
-
-    osend[...] = attended(1 - xl)
-    go(remote(osend, attg.at[hid, xl], xs.at[2], xr.at[2], pair))
-    attg[hid, xl] = attended(xl)
-    remote(osend, attg.at[hid, 1 - xl], xs.at[2], xr.at[2], pair).wait_recv()
+    loop2(lambda i: attend(block_at(4, i, 1 - c), (0,)))
+    hand_out(0)
+
+    def last(i, carry):
+        attend(lax.rem(z + 4, 8) * 4 + lax.rem(xl + i, 2) * 2 + lax.rem(c + i // 2, 2), (1,))
+        return carry
+
+    lax.fori_loop(0, 4, last, 0)
+    hand_out(1)
 
     own_w.wait()
     for d in range(1, 8):
@@ -270,19 +291,46 @@
         remote(wc.at[frm], wc.at[frm], ws.at[d], wr.at[d], at_head(frm)).wait_recv()
 
     fin = acc3.at[:, pl.ds(0, feat)]
-
-    def finish(stage):
-        def body(i, carry):
+    fin[...] = jnp.zeros((rows, feat), F32)
+
+    def finish(stage, qh):
+        def step(i, carry):
             p = piece_of(stage, i)
-            a = jnp.concatenate([attg[p, 0], attg[p, 1]], axis=1)
-            d = jnp.dot(a, wc[p], preferred_element_type=F32)
-            fin[...] += d
+            a = jnp.concatenate([attg[p, qh, 0], attg[p, qh, 1]], axis=1)
+            fin[pl.ds(qh * half, half), :] += jnp.dot(a, wc[p], preferred_element_type=F32)
             return carry
 
-        lax.fori_loop(0, 2, body, 0)
-
-    fin[...] = jnp.zeros((rows, feat), F32)
-    gather2(remote, go, attg, hid, hx, xh, y, x_partner, y_up, y_down, as_x, ar_x, as_y, ar_y, finish)
+        lax.fori_loop(0, 2, step, 0)
+
+    for qh in range(2):
+        slot = attg.at[hid, qh, 1 - xl]
+        remote(slot, slot, os.at[qh, 0], orr.at[qh, 0], pair).wait_recv()
+        whole = attg.at[hid, qh]
+        go(remote(whole, whole, ys.at[qh, 0], yr.at[qh, 0], y_up))
+        go(remote(whole, whole, ys.at[qh, 1], yr.at[qh, 1], y_down))
+        slot = attg.at[oid, qh, 1 - xl]
+        remote(slot, slot, os.at[qh, 1], orr.at[qh, 1], diag).wait_recv()
+        slot = attg.at[oid, qh, xl]
+        remote(slot, slot, os.at[qh, 2], orr.at[qh, 2], x_partner).wait_recv()
+        whole = attg.at[oid, qh]
+        go(remote(whole, whole, ys.at[qh, 2], yr.at[qh, 2], y_up))
+        go(remote(whole, whole, ys.at[qh, 3], yr.at[qh, 3], y_down))
+    finish(0, 0)
+    finish(0, 1)
+    for qh in range(2):
+        for g, xx in ((0, xh), (1, 1 - xh)):
+            lo, hi = attg.at[hx(xx, y - 1), qh], attg.at[hx(xx, y + 1), qh]
+            remote(lo, lo, ys.at[qh, 0], yr.at[qh, 2 * g], y_up).wait_recv()
+            go(remote(lo.at[0], lo.at[0], ys.at[qh, 4 + 2 * g], yr.at[qh, 4 + 2 * g], y_up))
+            remote(hi, hi, ys.at[qh, 1], yr.at[qh, 2 * g + 1], y_down).wait_recv()
+            go(remote(hi.at[1], hi.at[1], ys.at[qh, 5 + 2 * g], yr.at[qh, 5 + 2 * g], y_down))
+            finish(1 + g, qh)
+    for qh in range(2):
+        for g, xx in ((0, xh), (1, 1 - xh)):
+            far = attg.at[hx(xx, y + 2), qh]
+            remote(far.at[0], far.at[0], ys.at[qh, 4], yr.at[qh, 4 + 2 * g], y_up).wait_recv()
+            remote(far.at[1], far.at[1], ys.at[qh, 5], yr.at[qh, 5 + 2 * g], y_down).wait_recv()
+        finish(3, qh)
     out[...] = fin[...].astype(BF)
 
     for k in range(2, 7):
@@ -294,30 +342,6 @@
             remote(kv.at[0], kv.at[0], cs.at[d, k], cr.at[d, 0], twin).wait_send()
     for copy in pending:
         copy.wait_send()
-
-
-def gather2(remote, go, buf, hid, hx, xh, y, x_partner, y_up, y_down, sx, rx, sy, ry, consume):
-    mine, other = hx(xh, y), hx(1 - xh, y)
-    go(remote(buf.at[mine], buf.at[mine], sx.at[0], rx.at[0], x_partner))
-    go(remote(buf.at[mine], buf.at[mine], sy.at[0], ry.at[0], y_up))
-    go(remote(buf.at[mine], buf.at[mine], sy.at[1], ry.at[1], y_down))
-    remote(buf.at[other], buf.at[other], sx.at[0], rx.at[0], x_partner).wait_recv()
-    go(remote(buf.at[other], buf.at[other], sy.at[2], ry.at[2], y_up))
-    go(remote(buf.at[other], buf.at[other], sy.at[3], ry.at[3], y_down))
-    for g, xx in ((0, xh), (1, 1 - xh)):
-        lo, hi = hx(xx, y - 1), hx(xx, y + 1)
-        if g == 0:
-            consume(0)
-        remote(buf.at[lo], buf.at[lo], sy.at[0], ry.at[2 * g], y_up).wait_recv()
-        go(remote(buf.at[lo, 0], buf.at[lo, 0], sy.at[4 + 2 * g], ry.at[4 + 2 * g], y_up))
-        remote(buf.at[hi], buf.at[hi], sy.at[0], ry.at[2 * g + 1], y_down).wait_recv()
-        go(remote(buf.at[hi, 1], buf.at[hi, 1], sy.at[5 + 2 * g], ry.at[5 + 2 * g], y_down))
-        consume(1 + g)
-    for g, xx in ((0, xh), (1, 1 - xh)):
-        far = hx(xx, y + 2)
-        remote(buf.at[far, 0], buf.at[far, 0], sy.at[4], ry.at[4 + 2 * g], y_up).wait_recv()
-        remote(buf.at[far, 1], buf.at[far, 1], sy.at[5], ry.at[5 + 2 * g], y_down).wait_recv()
-    consume(3)
 
 
 def body(tokens, norm_gain, w_qkv, head_scale, w_out, scale_ids):
@@ -337,19 +361,19 @@
             pltpu.VMEM((3, dim, feat), BF),
             pltpu.VMEM((rows, 3 * feat), F32),
             pltpu.VMEM((rows, 128), F32),
-            pltpu.VMEM((32, 2, rows, 128), BF),
-            pltpu.VMEM((2, rows, 128), BF),
+            pltpu.VMEM((32, 2, 2, rows // 2, 128), BF),
+            pltpu.VMEM((2, 2, rows // 2, 128), BF),
             pltpu.VMEM((2, rows, 128), BF),
             pltpu.VMEM((rows, 128), BF),
             pltpu.VMEM((2, rows, 128), F32),
             pltpu.VMEM((2, rows, 128), F32),
             pltpu.VMEM((2, rows, 128), F32),
-            pltpu.VMEM((8, 2, rows, 128), BF),
-            pltpu.VMEM((rows, 128), BF),
+            pltpu.VMEM((8, 2, 2, rows // 2, 128), BF),
+            pltpu.VMEM((2, rows // 2, 128), BF),
             pltpu.VMEM((8, feat, feat), BF),
             dma((3,)),
             dma((1,)), dma((1,)), dma((8,)), dma((8,)),
-            dma((1,)), dma((1,)), dma((8,)), dma((8,)),
+            dma((2, 3)), dma((2, 3)), dma((2, 8)), dma((2, 8)),
             dma((8,)), dma((8,)),
             dma((3,)), dma((3,)),
             dma((2, 8)), dma((2, 8)),

time: 112 us -> 110 us (0.982); the launches traced: 112 us -> 108 us
  Pallas kernels: 110 us -> 106 us
    pallas_call x1, Pallas kernels: 110 us -> 106 us  [body(): pl.pallas_call(kernel, name='branch', out_shape=jax.ShapeDtypeStruct((row...]
where the time goes in v2:
time: 110 us; the launch traced here: 108 us
  Pallas kernels  106 us (96%)
  local copies, waits for them, and re-layouts  1.67 us (2%)
    pallas_call x1, Pallas kernels, body(): pl.pallas_call(kernel, name='branch', out_shape=jax.ShapeDtypeStruct((row...  106 us

profile of v2, /device:TPU:8, one launch (start us, length us, event | category | flops | bytes accessed | tf_op | source)
XLA Modules:
  0.0 108.0 jit_solution(3062057251480187524)
XLA Ops:
  0.0 106.4 %branch.1 = bf16[512,256]{1,0:T(8,128)(2,1)} custom-call(bf16[512,256]{1,0:T(8,128)(2,1)} %tokens.1, f32[1,2048]{1,0:T(1,128)} %bitcast.4, bf16[3,2048,256]{2,1,0:T(8,128)(2,1)} %wqkv.1, f32[1,2]{1,0:T(1,128)} %bitcast.5, bf16[256,2048]{1,0:T(8,128)(2,1)} %wout.1, s32[128,128]{1,0:T(8,128)} %bitcast.3), custom_call_target="tpu_custom_call" | custom-call | flops 11000000512 | bytes 6000000 | tf_op jit(solution)/shard_map/branch/pallas_call | solution.py:353
  106.4 1.7 %copy.8 = bf16[512,256]{1,0:T(8,128)(2,1)} copy(bf16[512,256]{1,0:T(8,128)(2,1)} %branch.1) | data formatting | bytes 524288

commit v3 on v2

--- a/solution.py
+++ b/solution.py
@@ -71,30 +71,18 @@
         pending.append(copy)
         return copy
 
-    def gather(first, buf, sx, rx, sy, ry, consume):
-        mine, other = hx(xh, y), hx(1 - xh, y)
-        half = rows // 2
-        top, bottom = pl.ds(0, half), pl.ds(half, half)
-        go(remote(first, buf.at[mine], sx.at[0], rx.at[0], x_partner))
-        go(remote(first, buf.at[mine], sy.at[0], ry.at[0], y_up))
-        go(remote(first, buf.at[mine], sy.at[1], ry.at[1], y_down))
-        remote(first, buf.at[other], sx.at[0], rx.at[0], x_partner).wait_recv()
-        go(remote(buf.at[other], buf.at[other], sy.at[2], ry.at[2], y_up))
-        go(remote(buf.at[other], buf.at[other], sy.at[3], ry.at[3], y_down))
-        for g, xx in ((0, xh), (1, 1 - xh)):
-            lo, hi = hx(xx, y - 1), hx(xx, y + 1)
-            if g == 0:
-                consume(0)
-            remote(buf.at[lo], buf.at[lo], sy.at[0], ry.at[2 * g], y_up).wait_recv()
-            go(remote(buf.at[lo, top], buf.at[lo, top], sy.at[4 + 2 * g], ry.at[4 + 2 * g], y_up))
-            remote(buf.at[hi], buf.at[hi], sy.at[0], ry.at[2 * g + 1], y_down).wait_recv()
-            go(remote(buf.at[hi, bottom], buf.at[hi, bottom], sy.at[5 + 2 * g], ry.at[5 + 2 * g], y_down))
-            consume(1 + g)
-        for g, xx in ((0, xh), (1, 1 - xh)):
-            far = hx(xx, y + 2)
-            remote(buf.at[far, top], buf.at[far, top], sy.at[4], ry.at[4 + 2 * g], y_up).wait_recv()
-            remote(buf.at[far, bottom], buf.at[far, bottom], sy.at[5], ry.at[5 + 2 * g], y_down).wait_recv()
-        consume(3)
+    half = rows // 2
+    mid = half // 2
+    oid = hx(1 - xh, y)
+
+    def part(ref, p, ch):
+        return ref.at[p, pl.ds(ch * half, half)]
+
+    for ch in range(2):
+        mine = tokens.at[pl.ds(ch * half, half)]
+        go(remote(mine, part(xg, hid, ch), gs_x.at[ch], gr_x.at[ch], x_partner))
+        go(remote(mine, part(xg, hid, ch), gs_y.at[ch, 0], gr_y.at[ch, 0], y_up))
+        go(remote(mine, part(xg, hid, ch), gs_y.at[ch, 1], gr_y.at[ch, 1], y_down))
 
     def piece_of(stage, i):
         if stage == 0:
@@ -112,56 +100,135 @@
     lacc[...] = jnp.zeros_like(lacc)
     acc3[...] = jnp.zeros_like(acc3)
     ssq[...] = jnp.zeros_like(ssq)
+
+    def project(stage, ch):
+        span = pl.ds(ch * half, half)
+
+        def step(i, carry):
+            p = piece_of(stage, i)
+            lane = pl.ds(pl.multiple_of(p * feat, feat), feat)
+            x = xg[p, span, :].astype(F32)
+            sqv = x * x
+            ssq[span, :] += sqv[:, :128] + sqv[:, 128:]
+            xw = (x * gain[:, lane]).astype(BF)
+            for j in range(3):
+                acc3[span, j * feat:(j + 1) * feat] += jnp.dot(xw, wq[j, lane, :], preferred_element_type=F32)
+            return carry
+
+        lax.fori_loop(0, 2, step, 0)
+
+    def pass_on(g, ch):
+        xx = xh if g == 0 else 1 - xh
+        lo, hi = hx(xx, y - 1), hx(xx, y + 1)
+        top = xg.at[lo, pl.ds(ch * half, mid)]
+        bottom = xg.at[hi, pl.ds(ch * half + mid, mid)]
+        remote(part(xg, lo, ch), part(xg, lo, ch), gs_y.at[ch, 0], gr_y.at[ch, 2 * g], y_up).wait_recv()
+        go(remote(top, top, gs_y.at[ch, 4 + 2 * g], gr_y.at[ch, 4 + 2 * g], y_up))
+        remote(part(xg, hi, ch), part(xg, hi, ch), gs_y.at[ch, 1], gr_y.at[ch, 2 * g + 1], y_down).wait_recv()
+        go(remote(bottom, bottom, gs_y.at[ch, 5 + 2 * g], gr_y.at[ch, 5 + 2 * g], y_down))
+
+    def far_in(ch):
+        for g, xx in ((0, xh), (1, 1 - xh)):
+            far = hx(xx, y + 2)
+            top = xg.at[far, pl.ds(ch * half, mid)]
+            bottom = xg.at[far, pl.ds(ch * half + mid, mid)]
+            remote(top, top, gs_y.at[ch, 4], gr_y.at[ch, 4 + 2 * g], y_up).wait_recv()
+            remote(bottom, bottom, gs_y.at[ch, 5], gr_y.at[ch, 5 + 2 * g], y_down).wait_recv()
+
+    for ch in range(2):
+        pass_on(0, ch)
+        slot = part(xg, oid, ch)
+        remote(slot, slot, gs_x.at[ch], gr_x.at[ch], x_partner).wait_recv()
+        go(remote(slot, slot, gs_y.at[ch, 2], gr_y.at[ch, 2], y_up))
+        go(remote(slot, slot, gs_y.at[ch, 3], gr_y.at[ch, 3], y_down))
     own.wait()
     loads.wait()
-
-    def project(stage):
-        def body(i, carry):
-            p = piece_of(stage, i)
-            lane = pl.ds(pl.multiple_of(p * feat, feat), feat)
-            x = xg[p].astype(F32)
-            sqv = x * x
-            ssq[...] += sqv[:, :128] + sqv[:, 128:]
-            xw = (x * gain[:, lane]).astype(BF)
-            for j in range(3):
-                acc3[:, j * feat:(j + 1) * feat] += jnp.dot(xw, wq[j, lane, :], preferred_element_type=F32)
-            return carry
-
-        lax.fori_loop(0, 2, body, 0)
-
-    gather(tokens, xg, gs_x, gr_x, gs_y, gr_y, project)
-
-    r = lax.rsqrt(jnp.sum(ssq[...], axis=-1, keepdims=True) * (1.0 / (8 * feat)) + 1e-06)
-
-    def head_of(j, h):
-        return acc3[:, pl.ds(pl.multiple_of(j * feat + h * hd_dim, hd_dim), hd_dim)] * r
+    project(0, 0)
+    project(1, 0)
+    pass_on(1, 0)
+    project(2, 0)
+    project(0, 1)
+    pass_on(1, 1)
 
     def unit(v, factor):
         power = jnp.sum(v * v, axis=-1, keepdims=True)
         return (v * lax.rsqrt(power + 1e-06) * factor).astype(BF)
 
-    half = rows // 2
-
-    def store(dst, j, value):
-        dst[0, j] = value[:half]
-        dst[1, j] = value[half:]
-
-    store(kv.at[sid], 0, unit(head_of(1, xl), 1.0))
-    store(kv.at[sid], 1, head_of(2, xl).astype(BF))
-    go(remote(kv.at[sid], kv.at[sid], zs.at[0, 0], zr.at[0, 0], z_up))
-    go(remote(kv.at[sid], kv.at[sid], zs.at[1, 0], zr.at[1, 0], z_down))
-    go(remote(kv.at[sid], kv.at[sid], cs.at[2, 0], cr.at[2, 0], twin))
-    store(kvsend, 0, unit(head_of(1, 1 - xl), 1.0))
-    store(kvsend, 1, head_of(2, 1 - xl).astype(BF))
-    go(remote(kvsend, kv.at[sid], xs.at[0], xr.at[0], pair))
-    qsend[...] = unit(head_of(0, 1 - xl), hscale[0, 1 - xl] * LOG2E)
-    go(remote(qsend, qbuf.at[xl], xs.at[1], xr.at[1], pair))
-    qbuf[xl] = unit(head_of(0, xl), hscale[0, xl] * LOG2E)
     other = sq(z, 1 - xl, c)
-    remote(kvsend, kv.at[other], xs.at[0], xr.at[0], pair).wait_recv()
-    go(remote(kv.at[other], kv.at[other], zs.at[0, 1], zr.at[0, 1], z_up))
-    go(remote(kv.at[other], kv.at[other], zs.at[1, 1], zr.at[1, 1], z_down))
-    go(remote(kv.at[other], kv.at[other], cs.at[2, 1], cr.at[2, 1], twin))
+
+    def ring_send(blk, ch, u):
+        it = kv.at[blk, ch]
+        go(remote(it, it, zs.at[0, ch, u], zr.at[0, ch, u], z_up))
+        go(remote(it, it, zs.at[1, ch, u], zr.at[1, ch, u], z_down))
+        go(remote(it, it, cs.at[2, ch, u], cr.at[2, ch, u], twin))
+
+    def heads(ch):
+        span = pl.ds(ch * half, half)
+        r = lax.rsqrt(jnp.sum(ssq[span, :], axis=-1, keepdims=True) * (1.0 / (8 * feat)) + 1e-06)
+
+        def head_of(j, h):
+            return acc3[span, pl.ds(pl.multiple_of(j * feat + h * hd_dim, hd_dim), hd_dim)] * r
+
+        kv[sid, ch, 0] = unit(head_of(1, xl), 1.0)
+        kv[sid, ch, 1] = head_of(2, xl).astype(BF)
+        ring_send(sid, ch, 0)
+        kvsend[ch, 0] = unit(head_of(1, 1 - xl), 1.0)
+        kvsend[ch, 1] = head_of(2, 1 - xl).astype(BF)
+        go(remote(kvsend.at[ch], kv.at[sid, ch], xs.at[ch, 0], xr.at[ch, 0], pair))
+        qsend[ch] = unit(head_of(0, 1 - xl), hscale[0, 1 - xl] * LOG2E)
+        go(remote(qsend.at[ch], qbuf.at[xl, span], xs.at[ch, 1], xr.at[ch, 1], pair))
+        qbuf[xl, span, :] = unit(head_of(0, xl), hscale[0, xl] * LOG2E)
+
+    far_in(0)
+    project(3, 0)
+    heads(0)
+    project(1, 1)
+    project(2, 1)
+    far_in(1)
+    project(3, 1)
+    heads(1)
+
+    def block_at(dz, u, cc):
+        return lax.rem(z + dz + 8, 8) * 4 + lax.rem(xl + u, 2) * 2 + cc
+
+    def to_twin(blk, d, ch, k):
+        return remote(kv.at[blk, ch], kv.at[blk, ch], cs.at[d, ch, k], cr.at[d, ch, k], twin)
+
+    def from_twin(blk, d, k):
+        for ch in range(2):
+            remote(kv.at[blk, ch], kv.at[blk, ch], cs.at[d, ch, 0], cr.at[d, ch, k], twin).wait_recv()
+
+    def landed(k, d, ch):
+        s, u = k // 2 + 1, lax.rem(k, 2)
+        blk = block_at(-s if d == 0 else s, u, c)
+        remote(kv.at[blk, ch], kv.at[blk, ch], zs.at[d, ch, 0], zr.at[d, ch, k], z_up).wait_recv()
+        return blk
+
+    def events(k, ch, d):
+        blk = landed(k, d, ch)
+        it = kv.at[blk, ch]
+        if d == 0:
+            @pl.when(k <= 4)
+            def _():
+                remote(it, it, zs.at[0, ch, k + 2], zr.at[0, ch, k + 2], z_up).start()
+        else:
+            @pl.when(k <= 3)
+            def _():
+                remote(it, it, zs.at[1, ch, k + 2], zr.at[1, ch, k + 2], z_down).start()
+
+            @pl.when(k == 5)
+            def _():
+                remote(it, it, zs.at[1, ch, k + 2], zr.at[1, ch, k + 2], z_down).start()
+        to_twin(blk, d, ch, k).start()
+
+    def pair_in(ch):
+        remote(kvsend.at[ch], kv.at[other, ch], xs.at[ch, 0], xr.at[ch, 0], pair).wait_recv()
+        ring_send(other, ch, 1)
+
+    pair_in(0)
+    events(0, 0, 0)
+    events(0, 0, 1)
+    pair_in(1)
 
     for d in range(1, 8):
         to = lax.rem(hid + d, 8)
@@ -169,7 +236,11 @@
             wout.at[:, pl.ds(pl.multiple_of(to * feat, feat), feat)], wc.at[hid],
             ws.at[d], wr.at[d], at_head(to),
         ))
-    remote(qsend, qbuf.at[1 - xl], xs.at[1], xr.at[1], pair).wait_recv()
+    events(0, 1, 0)
+    events(0, 1, 1)
+    for ch in range(2):
+        slot = qbuf.at[1 - xl, pl.ds(ch * half, half)]
+        remote(qsend.at[ch], slot, xs.at[ch, 1], xr.at[ch, 1], pair).wait_recv()
 
     def attend(blk, parts_of=(0, 1)):
         k = jnp.concatenate([kv[blk, 0, 0], kv[blk, 1, 0]], axis=0)
@@ -191,73 +262,35 @@
                 oacc[i, span, :] += jnp.dot(w, v, preferred_element_type=F32)
                 lacc[i, span, :] += total
 
-    def block_at(dz, u, cc):
-        return lax.rem(z + dz + 8, 8) * 4 + lax.rem(xl + u, 2) * 2 + cc
-
     def loop2(f):
         lax.fori_loop(0, 2, lambda i, carry: (f(i), carry)[1], 0)
-
-    def ring(k, d, dev_step):
-        s, u = k // 2 + 1, lax.rem(k, 2)
-        blk = block_at(-s if d == 0 else s, u, c)
-        remote(kv.at[blk], kv.at[blk], zs.at[d, 0], zr.at[d, k], z_up).wait_recv()
-        return blk
-
-    def to_twin(blk, d, k):
-        return remote(kv.at[blk], kv.at[blk], cs.at[d, k], cr.at[d, k], twin)
-
-    def from_twin(blk, d, k):
-        remote(kv.at[blk], kv.at[blk], cs.at[d, 0], cr.at[d, k], twin).wait_recv()
 
     loop2(lambda i: attend(block_at(0, i, c)))
     from_twin(block_at(0, 0, 1 - c), 2, 0)
     from_twin(block_at(0, 1, 1 - c), 2, 1)
+
+    def period(p, carry):
+        for ch in range(2):
+            events(p, ch, 0)
+            events(p, ch, 1)
+        s, u = (p + 1) // 2, lax.rem(p - 1, 2)
+        loop2(lambda i: attend(block_at((2 * i - 1) * s, u, c)))
+        from_twin(block_at(-s, u, 1 - c), 0, p - 1)
+        from_twin(block_at(s, u, 1 - c), 1, p - 1)
+        loop2(lambda i: attend(block_at((2 * i - 1) * s, u, 1 - c)))
+        return carry
+
     loop2(lambda i: attend(block_at(0, i, 1 - c)))
-
-    def lagged(k):
-        s, u = k // 2 + 1, lax.rem(k, 2)
-        from_twin(block_at(-s, u, 1 - c), 0, k)
-        from_twin(block_at(s, u, 1 - c), 1, k)
-        loop2(lambda i: attend(block_at((2 * i - 1) * s, u, 1 - c)))
-
-    def period(p, carry):
-        s, u = p // 2 + 1, lax.rem(p, 2)
-        up = ring(p, 0, z_up)
-
-        @pl.when(p <= 4)
-        def _():
-            remote(kv.at[up], kv.at[up], zs.at[0, p + 2], zr.at[0, p + 2], z_up).start()
-
-        to_twin(up, 0, p).start()
-        down = ring(p, 1, z_down)
-
-        @pl.when(p <= 3)
-        def _():
-            remote(kv.at[down], kv.at[down], zs.at[1, p + 2], zr.at[1, p + 2], z_down).start()
-
-        @pl.when(p == 5)
-        def _():
-            remote(kv.at[down], kv.at[down], zs.at[1, p + 2], zr.at[1, p + 2], z_down).start()
-
-        to_twin(down, 1, p).start()
-        loop2(lambda i: attend(block_at((2 * i - 1) * s, u, c)))
-
-        @pl.when(p > 0)
-        def _():
-            lagged(p - 1)
-
-        return carry
-
-    lax.fori_loop(0, 6, period, 0)
-    lagged(5)
-    last_up = block_at(4, 0, c)
-    last_down = block_at(4, 1, c)
-    remote(kv.at[last_up], kv.at[last_up], zs.at[0, 0], zr.at[0, 6], z_up).wait_recv()
-    go(to_twin(last_up, 0, 6))
-    remote(kv.at[last_down], kv.at[last_down], zs.at[1, 0], zr.at[1, 7], z_up).wait_recv()
-    go(to_twin(last_down, 1, 7))
-    oid = hx(1 - xh, y)
-
+    lax.fori_loop(1, 6, period, 0)
+    loop2(lambda i: attend(block_at((2 * i - 1) * 3, 1, c)))
+    for ch in range(2):
+        landed(6, 0, ch)
+        go(to_twin(block_at(4, 0, c), 0, ch, 6))
+        landed(7, 1, ch)
+        go(to_twin(block_at(4, 1, c), 1, ch, 7))
+    from_twin(block_at(-3, 1, 1 - c), 0, 5)
+    from_twin(block_at(3, 1, 1 - c), 1, 5)
+    loop2(lambda i: attend(block_at((2 * i - 1) * 3, 1, 1 - c)))
     def hand_out(qh):
         span = pl.ds(qh * half, half)
 
@@ -333,13 +366,15 @@
         finish(3, qh)
     out[...] = fin[...].astype(BF)
 
-    for k in range(2, 7):
-        remote(kv.at[0], kv.at[0], zs.at[0, k], zr.at[0, 0], z_up).wait_send()
-    for k in (2, 3, 4, 5, 7):
-        remote(kv.at[0], kv.at[0], zs.at[1, k], zr.at[1, 0], z_down).wait_send()
-    for k in range(6):
-        for d in range(2):
-            remote(kv.at[0], kv.at[0], cs.at[d, k], cr.at[d, 0], twin).wait_send()
+    it = kv.at[0, 0]
+    for ch in range(2):
+        for k in range(2, 7):
+            remote(it, it, zs.at[0, ch, k], zr.at[0, 0, 0], z_up).wait_send()
+        for k in (2, 3, 4, 5, 7):
+            remote(it, it, zs.at[1, ch, k], zr.at[1, 0, 0], z_down).wait_send()
+        for k in range(6):
+            for d in range(2):
+                remote(it, it, cs.at[d, ch, k], cr.at[d, 0, 0], twin).wait_send()
     for copy in pending:
         copy.wait_send()
 
@@ -364,7 +399,7 @@
             pltpu.VMEM((32, 2, 2, rows // 2, 128), BF),
             pltpu.VMEM((2, 2, rows // 2, 128), BF),
             pltpu.VMEM((2, rows, 128), BF),
-            pltpu.VMEM((rows, 128), BF),
+            pltpu.VMEM((2, rows // 2, 128), BF),
             pltpu.VMEM((2, rows, 128), F32),
             pltpu.VMEM((2, rows, 128), F32),
             pltpu.VMEM((2, rows, 128), F32),
@@ -372,12 +407,12 @@
             pltpu.VMEM((2, rows // 2, 128), BF),
             pltpu.VMEM((8, feat, feat), BF),
             dma((3,)),
-            dma((1,)), dma((1,)), dma((8,)), dma((8,)),
+            dma((2,)), dma((2,)), dma((2, 8)), dma((2, 8)),
             dma((2, 3)), dma((2, 3)), dma((2, 8)), dma((2, 8)),
             dma((8,)), dma((8,)),
-            dma((3,)), dma((3,)),
-            dma((2, 8)), dma((2, 8)),
-            dma((3, 8)), dma((3, 8)),
+            dma((2, 2)), dma((2, 2)),
+            dma((2, 2, 8)), dma((2, 2, 8)),
+            dma((3, 2, 8)), dma((3, 2, 8)),
         ],
         compiler_params=pltpu.CompilerParams(
             collective_id=0, has_side_effects=True, vmem_limit_bytes=56 * 1024 * 1024

time: 110 us -> 104 us (0.945); the launches traced: 108 us -> 104 us
  Pallas kernels: 106 us -> 102 us
    pallas_call x1, Pallas kernels: 106 us -> 102 us  [body(): pl.pallas_call(kernel, name='branch', out_shape=jax.ShapeDtypeStruct((row...]
where the time goes in v3:
time: 104 us
  Pallas kernels  102 us (98%)
  local copies, waits for them, and re-layouts  1.67 us (2%)
    pallas_call x1, Pallas kernels, body(): pl.pallas_call(kernel, name='branch', out_shape=jax.ShapeDtypeStruct((row...  102 us

profile of v3, /device:TPU:8, one launch (start us, length us, event | category | flops | bytes accessed | tf_op | source)
XLA Modules:
  0.0 103.8 jit_solution(1787724659950282114)
XLA Ops:
  0.0 102.1 %branch.1 = bf16[512,256]{1,0:T(8,128)(2,1)} custom-call(bf16[512,256]{1,0:T(8,128)(2,1)} %tokens.1, f32[1,2048]{1,0:T(1,128)} %bitcast.4, bf16[3,2048,256]{2,1,0:T(8,128)(2,1)} %wqkv.1, f32[1,2]{1,0:T(1,128)} %bitcast.5, bf16[256,2048]{1,0:T(8,128)(2,1)} %wout.1, s32[128,128]{1,0:T(8,128)} %bitcast.3), custom_call_target="tpu_custom_call" | custom-call | flops 11000000512 | bytes 6000000 | tf_op jit(solution)/shard_map/branch/pallas_call | solution.py:388
  102.1 1.7 %copy.8 = bf16[512,256]{1,0:T(8,128)(2,1)} copy(bf16[512,256]{1,0:T(8,128)(2,1)} %branch.1) | data formatting | bytes 524288

commit v4 on v3

--- a/solution.py
+++ b/solution.py
@@ -80,7 +80,7 @@
 
     for ch in range(2):
         mine = tokens.at[pl.ds(ch * half, half)]
-        go(remote(mine, part(xg, hid, ch), gs_x.at[ch], gr_x.at[ch], x_partner))
+        go(remote(mine, part(xg, hid, ch), gs_x.at[ch, 0], gr_x.at[ch, 0], x_partner))
         go(remote(mine, part(xg, hid, ch), gs_y.at[ch, 0], gr_y.at[ch, 0], y_up))
         go(remote(mine, part(xg, hid, ch), gs_y.at[ch, 1], gr_y.at[ch, 1], y_down))
 
@@ -127,28 +127,39 @@
         remote(part(xg, hi, ch), part(xg, hi, ch), gs_y.at[ch, 1], gr_y.at[ch, 2 * g + 1], y_down).wait_recv()
         go(remote(bottom, bottom, gs_y.at[ch, 5 + 2 * g], gr_y.at[ch, 5 + 2 * g], y_down))
 
-    def far_in(ch):
-        for g, xx in ((0, xh), (1, 1 - xh)):
-            far = hx(xx, y + 2)
+    def far_in(ch, *which):
+        for g in which:
+            far = hx(xh if g == 0 else 1 - xh, y + 2)
             top = xg.at[far, pl.ds(ch * half, mid)]
             bottom = xg.at[far, pl.ds(ch * half + mid, mid)]
             remote(top, top, gs_y.at[ch, 4], gr_y.at[ch, 4 + 2 * g], y_up).wait_recv()
             remote(bottom, bottom, gs_y.at[ch, 5], gr_y.at[ch, 5 + 2 * g], y_down).wait_recv()
 
-    for ch in range(2):
-        pass_on(0, ch)
-        slot = part(xg, oid, ch)
-        remote(slot, slot, gs_x.at[ch], gr_x.at[ch], x_partner).wait_recv()
-        go(remote(slot, slot, gs_y.at[ch, 2], gr_y.at[ch, 2], y_up))
-        go(remote(slot, slot, gs_y.at[ch, 3], gr_y.at[ch, 3], y_down))
+    def swap_in(p, ch, k):
+        slot = part(xg, p, ch)
+        remote(slot, slot, gs_x.at[ch, 0], gr_x.at[ch, k], x_partner).wait_recv()
+        return slot
+
+    def swap_out(p, ch, k):
+        slot = part(xg, p, ch)
+        go(remote(slot, slot, gs_x.at[ch, k], gr_x.at[ch, k], x_partner))
+
+    pass_on(0, 0)
+    slot = swap_in(oid, 0, 0)
+    go(remote(slot, slot, gs_y.at[0, 2], gr_y.at[0, 2], y_up))
+    go(remote(slot, slot, gs_y.at[0, 3], gr_y.at[0, 3], y_down))
+    pass_on(0, 1)
+    swap_out(hx(xh, y - 1), 1, 1)
+    swap_out(hx(xh, y + 1), 1, 2)
     own.wait()
     loads.wait()
     project(0, 0)
     project(1, 0)
     pass_on(1, 0)
     project(2, 0)
-    project(0, 1)
-    pass_on(1, 1)
+    project(1, 1)
+    far_in(1, 0)
+    swap_out(hx(xh, y + 2), 1, 3)
 
     def unit(v, factor):
         power = jnp.sum(v * v, axis=-1, keepdims=True)
@@ -179,12 +190,15 @@
         go(remote(qsend.at[ch], qbuf.at[xl, span], xs.at[ch, 1], xr.at[ch, 1], pair))
         qbuf[xl, span, :] = unit(head_of(0, xl), hscale[0, xl] * LOG2E)
 
-    far_in(0)
+    far_in(0, 0, 1)
     project(3, 0)
     heads(0)
-    project(1, 1)
+    swap_in(oid, 1, 0)
+    project(0, 1)
+    swap_in(hx(1 - xh, y - 1), 1, 1)
+    swap_in(hx(1 - xh, y + 1), 1, 2)
     project(2, 1)
-    far_in(1)
+    swap_in(hx(1 - xh, y + 2), 1, 3)
     project(3, 1)
     heads(1)
 
@@ -291,32 +305,64 @@
     from_twin(block_at(-3, 1, 1 - c), 0, 5)
     from_twin(block_at(3, 1, 1 - c), 1, 5)
     loop2(lambda i: attend(block_at((2 * i - 1) * 3, 1, 1 - c)))
-    def hand_out(qh):
+    def attended(i, qh):
         span = pl.ds(qh * half, half)
-
-        def attended(i):
-            total = jnp.sum(lacc[i, span, :], axis=-1, keepdims=True)
-            return (oacc[i, span, :] / total).astype(BF)
-
-        osend[qh] = attended(1 - xl)
-        mine = attg.at[hid, qh, xl]
-        go(remote(osend.at[qh], mine, os.at[qh, 0], orr.at[qh, 0], pair))
-        go(remote(osend.at[qh], mine, os.at[qh, 1], orr.at[qh, 1], diag))
-        attg[hid, qh, xl] = attended(xl)
-        go(remote(mine, mine, os.at[qh, 2], orr.at[qh, 2], x_partner))
+        total = jnp.sum(lacc[i, span, :], axis=-1, keepdims=True)
+        return (oacc[i, span, :] / total).astype(BF)
+
+    def over_x(qh, step, yy, theirs):
+        mine = attg.at[hx(xh, yy), qh, xl]
+        go(remote(theirs, mine, os.at[qh, step, 0], orr.at[qh, step, 0], pair))
+        go(remote(theirs, mine, os.at[qh, step, 1], orr.at[qh, step, 1], diag))
+        go(remote(mine, mine, os.at[qh, step, 2], orr.at[qh, step, 2], x_partner))
+
+    def from_x(qh, step, yy):
+        for k, (xx, hh, dev) in enumerate(((xh, 1 - xl, pair), (1 - xh, 1 - xl, diag), (1 - xh, xl, x_partner))):
+            slot = attg.at[hx(xx, yy), qh, hh]
+            remote(slot, slot, os.at[qh, 0, k], orr.at[qh, step, k], dev).wait_recv()
 
     loop2(lambda i: attend(block_at(4, i, c), (0,)))
     from_twin(block_at(4, 0, 1 - c), 0, 6)
     from_twin(block_at(4, 1, 1 - c), 1, 7)
     loop2(lambda i: attend(block_at(4, i, 1 - c), (0,)))
-    hand_out(0)
+    osend[y, 0] = attended(1 - xl, 0)
+    attg[hid, 0, xl] = attended(xl, 0)
+    over_x(0, 0, y, osend.at[y, 0])
 
     def last(i, carry):
         attend(lax.rem(z + 4, 8) * 4 + lax.rem(xl + i, 2) * 2 + lax.rem(c + i // 2, 2), (1,))
         return carry
 
     lax.fori_loop(0, 4, last, 0)
-    hand_out(1)
+    osend[y, 1] = attended(1 - xl, 1)
+    attg[hid, 1, xl] = attended(xl, 1)
+    theirs, ours = osend.at[y, 1], attg.at[hid, 1, xl]
+    for k, dev in enumerate((y_up, y_down)):
+        go(remote(theirs, theirs, ys.at[1, k], yr.at[1, k], dev))
+        go(remote(ours, ours, ys.at[1, 2 + k], yr.at[1, 2 + k], dev))
+    over_x(1, 0, y, theirs)
+
+    slot = attg.at[hid, 0, 1 - xl]
+    remote(slot, slot, os.at[0, 0, 0], orr.at[0, 0, 0], pair).wait_recv()
+    whole = attg.at[hid, 0]
+    go(remote(whole, whole, ys.at[0, 0], yr.at[0, 0], y_up))
+    go(remote(whole, whole, ys.at[0, 1], yr.at[0, 1], y_down))
+    lo, hi = lax.rem(y + 3, 4), lax.rem(y + 1, 4)
+    for k, yy in enumerate((lo, hi)):
+        theirs, ours = osend.at[yy, 1], attg.at[hx(xh, yy), 1, xl]
+        dev = (y_up, y_down)[k]
+        remote(theirs, theirs, ys.at[1, 0], yr.at[1, k], dev).wait_recv()
+        remote(ours, ours, ys.at[1, 0], yr.at[1, 2 + k], dev).wait_recv()
+        it = (theirs, ours)[k]
+        go(remote(it, it, ys.at[1, 4 + k], yr.at[1, 4 + k], dev))
+        over_x(1, 1 + k, yy, theirs)
+    slot = attg.at[oid, 0, 1 - xl]
+    remote(slot, slot, os.at[0, 0, 1], orr.at[0, 0, 1], diag).wait_recv()
+    slot = attg.at[oid, 0, xl]
+    remote(slot, slot, os.at[0, 0, 2], orr.at[0, 0, 2], x_partner).wait_recv()
+    whole = attg.at[oid, 0]
+    go(remote(whole, whole, ys.at[0, 2], yr.at[0, 2], y_up))
+    go(remote(whole, whole, ys.at[0, 3], yr.at[0, 3], y_down))
 
     own_w.wait()
     for d in range(1, 8):
@@ -335,35 +381,37 @@
 
         lax.fori_loop(0, 2, step, 0)
 
-    for qh in range(2):
-        slot = attg.at[hid, qh, 1 - xl]
-        remote(slot, slot, os.at[qh, 0], orr.at[qh, 0], pair).wait_recv()
-        whole = attg.at[hid, qh]
-        go(remote(whole, whole, ys.at[qh, 0], yr.at[qh, 0], y_up))
-        go(remote(whole, whole, ys.at[qh, 1], yr.at[qh, 1], y_down))
-        slot = attg.at[oid, qh, 1 - xl]
-        remote(slot, slot, os.at[qh, 1], orr.at[qh, 1], diag).wait_recv()
-        slot = attg.at[oid, qh, xl]
-        remote(slot, slot, os.at[qh, 2], orr.at[qh, 2], x_partner).wait_recv()
-        whole = attg.at[oid, qh]
-        go(remote(whole, whole, ys.at[qh, 2], yr.at[qh, 2], y_up))
-        go(remote(whole, whole, ys.at[qh, 3], yr.at[qh, 3], y_down))
     finish(0, 0)
+
+    def pass_half(g):
+        xx = xh if g == 0 else 1 - xh
+        lo, hi = attg.at[hx(xx, y - 1), 0], attg.at[hx(xx, y + 1), 0]
+        remote(lo, lo, ys.at[0, 0], yr.at[0, 2 * g], y_up).wait_recv()
+        go(remote(lo.at[0], lo.at[0], ys.at[0, 4 + 2 * g], yr.at[0, 4 + 2 * g], y_up))
+        remote(hi, hi, ys.at[0, 1], yr.at[0, 2 * g + 1], y_down).wait_recv()
+        go(remote(hi.at[1], hi.at[1], ys.at[0, 5 + 2 * g], yr.at[0, 5 + 2 * g], y_down))
+        finish(1 + g, 0)
+
+    pass_half(0)
+    far = lax.rem(y + 2, 4)
+    theirs, ours = osend.at[far, 1], attg.at[hx(xh, far), 1, xl]
+    remote(theirs, theirs, ys.at[1, 0], yr.at[1, 4], y_up).wait_recv()
+    remote(ours, ours, ys.at[1, 0], yr.at[1, 5], y_down).wait_recv()
+    over_x(1, 3, far, theirs)
+    pass_half(1)
+    from_x(1, 0, y)
     finish(0, 1)
-    for qh in range(2):
-        for g, xx in ((0, xh), (1, 1 - xh)):
-            lo, hi = attg.at[hx(xx, y - 1), qh], attg.at[hx(xx, y + 1), qh]
-            remote(lo, lo, ys.at[qh, 0], yr.at[qh, 2 * g], y_up).wait_recv()
-            go(remote(lo.at[0], lo.at[0], ys.at[qh, 4 + 2 * g], yr.at[qh, 4 + 2 * g], y_up))
-            remote(hi, hi, ys.at[qh, 1], yr.at[qh, 2 * g + 1], y_down).wait_recv()
-            go(remote(hi.at[1], hi.at[1], ys.at[qh, 5 + 2 * g], yr.at[qh, 5 + 2 * g], y_down))
-            finish(1 + g, qh)
-    for qh in range(2):
-        for g, xx in ((0, xh), (1, 1 - xh)):
-            far = attg.at[hx(xx, y + 2), qh]
-            remote(far.at[0], far.at[0], ys.at[qh, 4], yr.at[qh, 4 + 2 * g], y_up).wait_recv()
-            remote(far.at[1], far.at[1], ys.at[qh, 5], yr.at[qh, 5 + 2 * g], y_down).wait_recv()
-        finish(3, qh)
+    from_x(1, 1, lo)
+    from_x(1, 2, hi)
+    finish(1, 1)
+    finish(2, 1)
+    for g, xx in ((0, xh), (1, 1 - xh)):
+        piece = attg.at[hx(xx, y + 2), 0]
+        remote(piece.at[0], piece.at[0], ys.at[0, 4], yr.at[0, 4 + 2 * g], y_up).wait_recv()
+        remote(piece.at[1], piece.at[1], ys.at[0, 5], yr.at[0, 5 + 2 * g], y_down).wait_recv()
+    finish(3, 0)
+    from_x(1, 3, far)
+    finish(3, 1)
     out[...] = fin[...].astype(BF)
 
     it = kv.at[0, 0]
@@ -404,11 +452,11 @@
             pltpu.VMEM((2, rows, 128), F32),
             pltpu.VMEM((2, rows, 128), F32),
             pltpu.VMEM((8, 2, 2, rows // 2, 128), BF),
-            pltpu.VMEM((2, rows // 2, 128), BF),
+            pltpu.VMEM((4, 2, rows // 2, 128), BF),
             pltpu.VMEM((8, feat, feat), BF),
             dma((3,)),
-            dma((2,)), dma((2,)), dma((2, 8)), dma((2, 8)),
-            dma((2, 3)), dma((2, 3)), dma((2, 8)), dma((2, 8)),
+            dma((2, 4)), dma((2, 4)), dma((2, 8)), dma((2, 8)),
+            dma((2, 4, 3)), dma((2, 4, 3)), dma((2, 8)), dma((2, 8)),
             dma((8,)), dma((8,)),
             dma((2, 2)), dma((2, 2)),
             dma((2, 2, 8)), dma((2, 2, 8)),

time: 104 us -> 100 us (0.962)
  Pallas kernels: 102 us -> 98.4 us
    pallas_call x1, Pallas kernels: 102 us -> 98.4 us  [body(): pl.pallas_call(kernel, name='branch', out_shape=jax.ShapeDtypeStruct((row...]
where the time goes in v4:
time: 100 us
  Pallas kernels  98.4 us (98%)
  local copies, waits for them, and re-layouts  1.67 us (2%)
    pallas_call x1, Pallas kernels, body(): pl.pallas_call(kernel, name='branch', out_shape=jax.ShapeDtypeStruct((row...  98.4 us

profile of v4, /device:TPU:8, one launch (start us, length us, event | category | flops | bytes accessed | tf_op | source)
XLA Modules:
  0.0 100.1 jit_solution(2194632926698844525)
XLA Ops:
  0.0 98.4 %branch.1 = bf16[512,256]{1,0:T(8,128)(2,1)} custom-call(bf16[512,256]{1,0:T(8,128)(2,1)} %tokens.1, f32[1,2048]{1,0:T(1,128)} %bitcast.4, bf16[3,2048,256]{2,1,0:T(8,128)(2,1)} %wqkv.1, f32[1,2]{1,0:T(1,128)} %bitcast.5, bf16[256,2048]{1,0:T(8,128)(2,1)} %wout.1, s32[128,128]{1,0:T(8,128)} %bitcast.3), custom_call_target="tpu_custom_call" | custom-call | flops 11000000512 | bytes 6000000 | tf_op jit(solution)/shard_map/branch/pallas_call | solution.py:436
  98.4 1.7 %copy.8 = bf16[512,256]{1,0:T(8,128)(2,1)} copy(bf16[512,256]{1,0:T(8,128)(2,1)} %branch.1) | data formatting | bytes 524288
